TPU v7x, 32 devices: a whole 2x2x4 slice. The times are simulated.
32 devices in a mesh: groups: 2 (over y), seq: 4 (over z), tensor: 2 (over x), sub: 2 (over core).
Axes of the slice: x: 2, y: 2, z: 4, core: 2. Of those that a mesh axis runs over, the one named last changes fastest.
Arguments:
- activations: bfloat16 [4096, 4096], P(('groups', 'seq'), ('tensor', 'sub')), parts along dimension 0, may hold values from -18 to 18
- conv_weight: bfloat16 [512, 4096], P(None, ('tensor', 'sub')), may hold values from -0.25 to 0.25
- query_weight: bfloat16 [4096, 2048], P('seq', ('tensor', 'sub')), may hold values from -0.09375 to 0.09375
- key_weight: bfloat16 [4096, 2048], P('seq', ('tensor', 'sub')), may hold values from -0.09375 to 0.09375
- value_weight: bfloat16 [4096, 2048], P('seq', ('tensor', 'sub')), may hold values from -0.09375 to 0.09375
- segment_for_slot: int32 [16], P('groups'), parts along dimension 0, may hold values from 0 to 7, each once
- book_length: int32 [2], P('groups'), parts along dimension 0, may hold values from 1024 to 2048
Outputs:
- context: bfloat16 [4096, 2048], P(('groups', 'seq'), ('tensor', 'sub')), parts along dimension 0
There are 2 independent parts, one for each index of `groups`. A program takes and returns all parts, laid end to end along the dimension named above; an argument that names none is the same for every part. Nothing has to cross between parts.
Inputs may be any that keep to these rules, and one draw needn't show every extreme that they name: `segment_for_slot`: each segment appears in exactly one slot.
All inputs are finite; a program needn't handle non-finite values.
Results may differ from a plain program's by a relative error of at most 0.012.
The roundings to bfloat16 on the way count: a program that leaves them out, or rounds other values in their place, can miss the bound.
Values may be sent and summed in bfloat16 or wider, within the bound.
No kernel may reach another device: no remote copies, remote signals or barrier semaphores. Data moves between devices by JAX's collectives and lax.ppermute only.
A program may use at most 64 MiB of HBM per device.

v0:
```python
import jax
import jax.numpy as jnp
from jax import lax
from jax.sharding import PartitionSpec as P

HD = 128
CG = 128
RATE = 4
SLOTS = 2
SEG = 256
MEM = 64


def compress_rows(local_rows, conv_local):
    count_rows, channels = local_rows.shape
    groups = channels // CG
    shaped = local_rows.reshape(count_rows // RATE, RATE, groups, CG)
    kernel = conv_local.reshape(RATE, CG, groups, CG)
    mixed_out = jnp.einsum("mtgc,tcgo->mgo", shaped, kernel, preferred_element_type=jnp.float32)
    return mixed_out.reshape(count_rows // RATE, channels).astype(jnp.bfloat16)


def add_product(source, weight_rows):
    return jnp.dot(source, weight_rows, preferred_element_type=jnp.float32)


def local_attention(queries, keys_here, values_here):
    total_rows, head_count, head_dim = queries.shape
    slot_count = total_rows // SEG
    shaped_q = queries.reshape(slot_count, SEG, head_count, head_dim)
    shaped_k = keys_here.reshape(slot_count, SEG, head_count, head_dim)
    shaped_v = values_here.reshape(slot_count, SEG, head_count, head_dim)
    scores = jnp.einsum(
        "asnd,atnd->asnt", shaped_q, shaped_k, preferred_element_type=jnp.float32
    ) * HD ** (-0.5)
    causal = jnp.arange(SEG, dtype=jnp.int32)[:, None] >= jnp.arange(SEG, dtype=jnp.int32)[None, :]
    scores = jnp.where(causal[None, :, None, :], scores, -jnp.inf)
    row_best = jnp.max(scores, axis=3)
    weights = jnp.exp(scores - row_best[..., None])
    denominator = jnp.sum(weights, axis=3)
    weighted_numerator = jnp.einsum(
        "asnt,atnd->asnd",
        weights.astype(jnp.bfloat16),
        shaped_v,
        preferred_element_type=jnp.float32,
    )
    return (
        row_best.reshape(total_rows, head_count),
        denominator.reshape(total_rows, head_count),
        weighted_numerator.reshape(total_rows, head_count, head_dim),
    )


def memory_step(state, pieces, queries, row_segment, segment_for_slot):
    keys_in, values_in = pieces
    count_keys = keys_in.shape[0]
    total_rows, head_count, head_dim = queries.shape
    key_slot = jnp.arange(count_keys, dtype=jnp.int32) // MEM
    slot_ids = jnp.arange(segment_for_slot.shape[0], dtype=jnp.int32)
    key_segment = jnp.sum(
        jnp.where(key_slot[:, None] == slot_ids[None, :], segment_for_slot[None, :], 0), axis=1
    )
    row_best, denominator, weighted_numerator = state
    shaped_keys = keys_in.reshape(count_keys, head_count, head_dim)
    shaped_values = values_in.reshape(count_keys, head_count, head_dim)
    scores = jnp.einsum(
        "rnd,knd->rnk", queries, shaped_keys, preferred_element_type=jnp.float32
    ) * HD ** (-0.5)
    allowed = key_segment[None, None, :] < row_segment[:, None, None]
    scores = jnp.where(allowed, scores, -jnp.inf)
    new_best = jnp.maximum(row_best, jnp.max(scores, axis=2))
    weights = jnp.exp(scores - new_best[:, :, None])
    factor = jnp.exp(row_best - new_best)
    denominator = denominator * factor + jnp.sum(weights, axis=2)
    weighted_numerator = weighted_numerator * factor[:, :, None] + jnp.einsum(
        "rnk,knd->rnd",
        weights.astype(jnp.bfloat16),
        shaped_values,
        preferred_element_type=jnp.float32,
    )
    return (new_best, denominator, weighted_numerator)


def on_device(
    activations, conv_weight, query_weight, key_weight, value_weight, segment_for_slot, book_length
):
    compressed_local = compress_rows(activations, conv_weight)
    full_rows, full_compressed = (
        lax.all_gather(activations, ("tensor", "sub"), axis=1, tiled=True),
        lax.all_gather(compressed_local, ("tensor", "sub"), axis=1, tiled=True),
    )
    total_rows = full_rows.shape[0]
    local_width = query_weight.shape[1]
    head_count = local_width // HD
    shard_index = lax.axis_index("seq")
    my_segments = lax.dynamic_slice_in_dim(segment_for_slot, shard_index * SLOTS, SLOTS, 0)
    row_segment = jnp.repeat(my_segments, SEG, total_repeat_length=total_rows)
    query_rows = lax.all_gather(query_weight, "seq", axis=0, tiled=True)
    key_matrix_rows = lax.all_gather(key_weight, "seq", axis=0, tiled=True)
    value_rows = lax.all_gather(value_weight, "seq", axis=0, tiled=True)
    queries = add_product(full_rows, query_rows).astype(jnp.bfloat16)
    keys_here = add_product(full_rows, key_matrix_rows).astype(jnp.bfloat16)
    values_here = add_product(full_rows, value_rows).astype(jnp.bfloat16)
    keys_mem = add_product(full_compressed, key_matrix_rows).astype(jnp.bfloat16)
    values_mem = add_product(full_compressed, value_rows).astype(jnp.bfloat16)
    shaped_q = queries.reshape(total_rows, head_count, HD)
    state = local_attention(
        shaped_q,
        keys_here.reshape(total_rows, head_count, HD),
        values_here.reshape(total_rows, head_count, HD),
    )
    state = memory_step(
        state,
        (
            lax.all_gather(keys_mem, "seq", axis=0, tiled=True),
            lax.all_gather(values_mem, "seq", axis=0, tiled=True),
        ),
        shaped_q,
        row_segment,
        segment_for_slot,
    )
    row_best, denominator, weighted_numerator = state
    result = (weighted_numerator / denominator[:, :, None]).reshape(total_rows, local_width)
    position = row_segment * SEG + jnp.arange(total_rows, dtype=jnp.int32) % SEG
    result = jnp.where((position < book_length[0])[:, None], result, 0.0)
    return result.astype(jnp.bfloat16)


def solution(mesh):
    placed = (
        P(("groups", "seq"), ("tensor", "sub")),
        P(None, ("tensor", "sub")),
        P("seq", ("tensor", "sub")),
        P("seq", ("tensor", "sub")),
        P("seq", ("tensor", "sub")),
        P("groups"),
        P("groups"),
    )
    return jax.shard_map(
        on_device,
        mesh=mesh,
        in_specs=placed,
        out_specs=P(("groups", "seq"), ("tensor", "sub")),
        check_vma=False,
    )
```

profile of v0, /device:TPU:0, one launch (start us, length us, event | category | flops | bytes accessed | tf_op | source)
XLA Modules:
  0.0 350.5 jit_solution(3054702752094949203)
XLA Ops:
  6.5 0.0 copy-start
  6.5 0.0 all-gather.6.cloned.1.call-start
  6.5 0.7 all-gather.6.cloned.1.call-update
  7.3 0.0 all-gather.10.cloned.1.call-start
  7.3 0.7 all-gather.10.cloned.1.call-update
  8.0 0.0 all-gather.12.cloned.1.call-start
  8.1 0.7 all-gather.12.cloned.1.call-update
  8.7 0.0 all-gather.14.cloned.1.call-start
  8.8 0.0 copy-start.5
  8.8 0.0 copy-start.4
  8.8 1.5 copy.64
  10.3 0.0 copy-done
  10.3 0.3 copy.65
  10.6 1.7 fusion.17
  12.3 0.0 all-gather.14.cloned.1.call-update
  12.3 0.0 all-gather.8.cloned.1.call-start
  12.4 0.5 all-gather.8.cloned.1.call-update
  13.5 0.0 copy-done.5
  13.6 0.1 dynamic_slice.3
  13.6 0.6 fusion.41
  14.2 0.1 select_reduce_fusion
  14.3 0.0 copy-done.4
  14.3 1.3 fusion.32
  15.6 1.3 broadcast_select_fusion
  16.9 0.2 broadcast_compare_fusion
  17.1 29.0 %all-gather.6.cloned.1.call-done = bf16[512,4096]{1,0:T(8,128)(2,1)} async-done(((bf16[512,1024]{1,0:T(8,128)(2,1)}), bf16[512,4096]{1,0:T(8,128)(2,1)}) %all-gather.6.cloned.1.call-update) | async-done | bytes 4194320 | tf_op jit(solution)/shard_map/all_gather | solution.py:89
  46.1 82.4 %all-gather.10.cloned.1.call-done = bf16[4096,512]{1,0:T(8,128)(2,1)} async-done(((bf16[1024,512]{1,0:T(8,128)(2,1)}), bf16[4096,512]{1,0:T(8,128)(2,1)}) %all-gather.10.cloned.1.call-update) | async-done | bytes 4194320 | tf_op jit(solution)/shard_map/all_gather | solution.py:99
  128.5 5.8 %convolution_convert_fusion.1 = bf16[512,512]{1,0:T(8,128)(2,1)S(1)} fusion(bf16[512,4096]{1,0:T(8,128)(2,1)} %all-gather.6.cloned.1.call-done, bf16[4096,512]{1,0:T(8,128)(2,1)} %all-gather.10.cloned.1.call-done), kind=kOutput, calls=%fused_computation.18 | convolution fusion | flops 2147745792 | bytes 8912896 | tf_op jit(solution)/shard_map/dot_general | solution.py:24
  134.3 0.1 reshape_reshape.10
  134.4 75.0 %all-gather.12.cloned.1.call-done = bf16[4096,512]{1,0:T(8,128)(2,1)} async-done(((bf16[1024,512]{1,0:T(8,128)(2,1)}), bf16[4096,512]{1,0:T(8,128)(2,1)}) %all-gather.12.cloned.1.call-update) | async-done | bytes 4194320 | tf_op jit(solution)/shard_map/all_gather | solution.py:98
  209.4 5.8 %convolution_convert_fusion = bf16[512,512]{0,1:T(8,128)(2,1)S(1)} fusion(bf16[512,4096]{1,0:T(8,128)(2,1)} %all-gather.6.cloned.1.call-done, bf16[4096,512]{1,0:T(8,128)(2,1)} %all-gather.12.cloned.1.call-done), kind=kOutput, calls=%fused_computation.17 | convolution fusion | flops 2147745792 | bytes 8912896 | tf_op jit(solution)/shard_map/dot_general | solution.py:24
  215.2 0.0 copy-start.3
  215.3 0.1 reshape_reshape.11
  215.4 10.7 %all-gather.14.cloned.1.call-done = bf16[128,4096]{0,1:T(8,128)(2,1)} async-done(((bf16[128,1024]{0,1:T(8,128)(2,1)}), bf16[128,4096]{0,1:T(8,128)(2,1)}) %all-gather.14.cloned.1.call-update) | async-done | bytes 1048592 | tf_op jit(solution)/shard_map/all_gather | solution.py:90
  226.1 3.3 convolution_convert_fusion.4
  229.4 21.4 %all_gather.26 = bf16[512,512]{1,0:T(8,128)(2,1)} all-gather(bf16[128,512]{1,0:T(8,128)(2,1)S(1)} %convolution_convert_fusion.4), channel_id=1, replica_groups=mesh['groups'=2,'seq'=4,'tensor'=2,'sub'=2] {'seq'}, dimensions={0}, use_global_device_ids=true | all-gather | bytes 655360 | tf_op jit(solution)/shard_map/all_gather | solution.py:115
  250.8 61.4 %all-gather.8.cloned.1.call-done = bf16[4096,512]{1,0:T(8,128)(2,1)} async-done(((bf16[1024,512]{1,0:T(8,128)(2,1)}), bf16[4096,512]{1,0:T(8,128)(2,1)}) %all-gather.8.cloned.1.call-update) | async-done | bytes 4194320 | tf_op jit(solution)/shard_map/all_gather | solution.py:100
  312.2 0.0 copy-done.3
  312.2 5.8 %convolution_convert_fusion.2 = bf16[512,512]{1,0:T(8,128)(2,1)S(1)} fusion(bf16[512,4096]{1,0:T(8,128)(2,1)} %all-gather.6.cloned.1.call-done, bf16[4096,512]{1,0:T(8,128)(2,1)} %all-gather.8.cloned.1.call-done), kind=kOutput, calls=%fused_computation.19 | convolution fusion | flops 2147745792 | bytes 8912896 | tf_op jit(solution)/shard_map/dot_general | solution.py:24
  318.0 0.1 reshape_reshape.9
  318.1 0.5 fusion.42
  318.6 0.3 fusion.9
  318.9 0.0 copy-start.1
  318.9 0.5 convolution_bitcast_fusion
  319.4 0.3 copy.49
  319.7 0.3 copy.54
  320.1 0.0 copy-done.1
  320.1 0.0 copy-start.2
  320.1 3.0 convolution_convert_fusion.3
  323.1 15.2 %all_gather.27 = bf16[512,512]{1,0:T(8,128)(2,1)S(1)} all-gather(bf16[128,512]{1,0:T(8,128)(2,1)S(1)} %convolution_convert_fusion.3), channel_id=1, replica_groups=mesh['groups'=2,'seq'=4,'tensor'=2,'sub'=2] {'seq'}, dimensions={0}, use_global_device_ids=true | all-gather | bytes 655360 | tf_op jit(solution)/shard_map/all_gather | solution.py:116
  338.4 0.2 copy.62
  338.6 0.0 copy-done.2
  338.6 1.9 fusion.2
  340.5 0.9 fusion
  341.4 1.4 fusion.22
  342.8 0.2 copy.57
  343.0 1.0 select_convert_fusion
  (4 shorter events, 0.0 us)
Async XLA Ops:
  6.5 3.8 %copy-start = (bf16[512,1024]{1,0:T(8,128)(2,1)S(1)}, bf16[512,1024]{1,0:T(8,128)(2,1)}, u32[]{:S(2)}) copy-start(bf16[512,1024]{1,0:T(8,128)(2,1)} %param.9) | copy-start | bytes 3145732
  6.5 39.6 %all-gather.6.cloned.1.call-start = ((), (), s32[]{:S(2)}) async-start(), calls=%async_computation | async-start | bytes 5242880 | tf_op jit(solution)/shard_map/all_gather | solution.py:89
  7.3 121.2 %all-gather.10.cloned.1.call-start = ((), (), s32[]{:S(2)}) async-start(), calls=%async_computation.2 | async-start | bytes 5242880 | tf_op jit(solution)/shard_map/all_gather | solution.py:99
  8.0 201.4 %all-gather.12.cloned.1.call-start = ((), (), s32[]{:S(2)}) async-start(), calls=%async_computation.3 | async-start | bytes 5242880 | tf_op jit(solution)/shard_map/all_gather | solution.py:98
  8.7 217.4 %all-gather.14.cloned.1.call-start = ((), (), s32[]{:S(2)}) async-start(), calls=%async_computation.4 | async-start | bytes 1310720 | tf_op jit(solution)/shard_map/all_gather | solution.py:90
  8.8 4.8 %copy-start.5 = (s32[8]{0:T(128)S(1)}, s32[8]{0:T(128)}, u32[]{:S(2)}) copy-start(s32[8]{0:T(128)} %param.14) | copy-start | bytes 100
  8.8 5.5 %copy-start.4 = (pred[512]{0:T(512)(128)(4,1)S(1)}, pred[512]{0:T(512)(128)(4,1)}, u32[]{:S(2)}) copy-start(pred[512]{0:T(512)(128)(4,1)} %constant.157) | copy-start | bytes 1540
  12.3 299.9 %all-gather.8.cloned.1.call-start = ((), (), s32[]{:S(2)}) async-start(), calls=%async_computation.1 | async-start | bytes 5242880 | tf_op jit(solution)/shard_map/all_gather | solution.py:100
  215.2 96.9 %copy-start.3 = (bf16[512,512]{0,1:T(8,128)(2,1)}, bf16[512,512]{0,1:T(8,128)(2,1)S(1)}, u32[]{:S(2)}) copy-start(bf16[512,512]{0,1:T(8,128)(2,1)S(1)} %convolution_convert_fusion) | copy-start | bytes 1572868
  318.9 1.2 copy-start.1
  320.1 18.4 %copy-start.2 = (bf16[512,512]{1,0:T(8,128)(2,1)S(1)}, bf16[512,512]{1,0:T(8,128)(2,1)}, u32[]{:S(2)}) copy-start(bf16[512,512]{1,0:T(8,128)(2,1)} %all_gather.26) | copy-start | bytes 1572868
Sparse Core Ops, SparseCore 0:
  8.9 37.1 all-gather.5
  47.7 80.7 all-gather.9
  130.1 79.2 all-gather.11
  210.8 15.2 all-gather.13
  227.5 84.6 all-gather.7
where the time goes:
time: 351 us
  waiting for transfers between devices  261 us (74%)
  blocking collectives  36.6 us (10%)
  matrix products  29.6 us (8%)
  between operations  14 us (4%)
  other arithmetic  5.11 us (1%)
  local copies, waits for them, and re-layouts  3.95 us (1%)
    all_gather x1, waiting for transfers between devices, on_device(): key_matrix_rows = lax.all_gather(key_weight, 'seq', axis=0, tiled=True)  82.4 us
    all_gather x1, waiting for transfers between devices, on_device(): query_rows = lax.all_gather(query_weight, 'seq', axis=0, tiled=True)  75 us
    all_gather x1, waiting for transfers between devices, on_device(): value_rows = lax.all_gather(value_weight, 'seq', axis=0, tiled=True)  61.4 us
    all_gather x1, waiting for transfers between devices, on_device(): lax.all_gather(activations, ('tensor', 'sub'), axis=1, tiled=True)  29 us
    dot_general x5, matrix products, add_product(): return jnp.dot(source, weight_rows, preferred_element_type=jnp.float32)  23.6 us
    all_gather x1, blocking collectives, on_device(): lax.all_gather(keys_mem, 'seq', axis=0, tiled=True)  21.4 us
    all_gather x1, blocking collectives, on_device(): lax.all_gather(values_mem, 'seq', axis=0, tiled=True)  15.2 us
    all_gather x1, waiting for transfers between devices, on_device(): lax.all_gather(compressed_local, ('tensor', 'sub'), axis=1, tiled=True)  10.7 us
  transfers between devices with their start and end apart: 5, of which 5 were waited for; matrix products, arithmetic and copies ran while one was open for 6% of the time, Pallas kernels for 0%

commit v1 on v0

--- a/solution.py
+++ b/solution.py
@@ -96,7 +96,35 @@
     my_segments = lax.dynamic_slice_in_dim(segment_for_slot, shard_index * SLOTS, SLOTS, 0)
     row_segment = jnp.repeat(my_segments, SEG, total_repeat_length=total_rows)
     query_rows = lax.all_gather(query_weight, "seq", axis=0, tiled=True)
-    key_matrix_rows = lax.all_gather(key_weight, "seq", axis=0, tiled=True)
+    earlier, right_arr, lower = (
+        jax.lax.axis_size("seq"),
+        jax.lax.axis_index("seq"),
+        key_weight.shape[0],
+    )
+    cards = []
+    for dev_j in range(earlier):
+        cards.append((dev_j, (dev_j + 1) % earlier))
+    all_rows = []
+    for dev_j in range(earlier):
+        all_rows.append((dev_j, (dev_j - 1) % earlier))
+    key_matrix_rows = jnp.zeros(
+        (*key_weight.shape[:0], earlier * lower, *key_weight.shape[1:]), key_weight.dtype
+    )
+    key_matrix_rows = lax.dynamic_update_slice_in_dim(
+        key_matrix_rows, key_weight, right_arr * lower, axis=0
+    )
+    w_next = x_new = key_weight
+    s_next = earlier // 2
+    for dd in range(1, s_next + 1):
+        w_next = jax.lax.ppermute(w_next, "seq", cards)
+        key_matrix_rows = lax.dynamic_update_slice_in_dim(
+            key_matrix_rows, w_next, (right_arr - dd) % earlier * lower, axis=0
+        )
+        if dd < earlier - s_next:
+            x_new = jax.lax.ppermute(x_new, "seq", all_rows)
+            key_matrix_rows = lax.dynamic_update_slice_in_dim(
+                key_matrix_rows, x_new, (right_arr + dd) % earlier * lower, axis=0
+            )
     value_rows = lax.all_gather(value_weight, "seq", axis=0, tiled=True)
     queries = add_product(full_rows, query_rows).astype(jnp.bfloat16)
     keys_here = add_product(full_rows, key_matrix_rows).astype(jnp.bfloat16)

time: 351 us -> 284 us (0.81)
  waiting for transfers between devices: 261 us -> 171 us
  blocking collectives: 36.6 us -> 47.6 us
  local copies, waits for them, and re-layouts: 3.95 us -> 11.8 us
  starting transfers between devices: 0.16 us -> 5.29 us
    all_gather x1 -> x0, waiting for transfers between devices: 82.4 us -> none  [on_device(): key_matrix_rows = lax.all_gather(key_weight, 'seq', axis=0, tiled=True)]
    ppermute x0 -> x3, waiting for transfers between devices: none -> 65.9 us  [the longest x2 49.1 us: on_device(): w_next = jax.lax.ppermute(w_next, 'seq', cards)]
    all_gather x1, waiting for transfers between devices: 75 us -> 27.4 us  [on_device(): query_rows = lax.all_gather(query_weight, 'seq', axis=0, tiled=True)]
    all_gather x1, waiting for transfers between devices: 29 us -> 0.01 us  [on_device(): lax.all_gather(activations, ('tensor', 'sub'), axis=1, tiled=True)]
    all_gather x1, waiting for transfers between devices: 61.4 us -> 75.4 us  [on_device(): value_rows = lax.all_gather(value_weight, 'seq', axis=0, tiled=True)]
    all_gather x1, waiting for transfers between devices: 10.7 us -> 0.01 us  [on_device(): lax.all_gather(compressed_local, ('tensor', 'sub'), axis=1, tiled=True)]
    all_gather x1, blocking collectives: 21.4 us -> 31.2 us  [on_device(): lax.all_gather(keys_mem, 'seq', axis=0, tiled=True)]
    ppermute x0 -> x3, starting transfers between devices: none -> 5.17 us  [the longest x2 3.08 us: on_device(): w_next = jax.lax.ppermute(w_next, 'seq', cards)]
  transfers between devices with their start and end apart: 5 -> 7, of which waited for: 5 -> 5; matrix products, arithmetic and copies ran while one was open for 6% -> 9% of each run, Pallas kernels for 0% -> 0%
where the time goes in v1:
time: 284 us
  waiting for transfers between devices  171 us (60%)
  blocking collectives  47.6 us (17%)
  matrix products  29.7 us (10%)
  between operations  14 us (5%)
  local copies, waits for them, and re-layouts  11.8 us (4%)
  starting transfers between devices  5.29 us (2%)
  other arithmetic  5.15 us (2%)
    all_gather x1, waiting for transfers between devices, on_device(): value_rows = lax.all_gather(value_weight, 'seq', axis=0, tiled=True)  75.4 us
    ppermute x2, waiting for transfers between devices, on_device(): w_next = jax.lax.ppermute(w_next, 'seq', cards)  49.1 us
    all_gather x1, blocking collectives, on_device(): lax.all_gather(keys_mem, 'seq', axis=0, tiled=True)  31.2 us
    all_gather x1, waiting for transfers between devices, on_device(): query_rows = lax.all_gather(query_weight, 'seq', axis=0, tiled=True)  27.4 us
    dot_general x5, matrix products, add_product(): return jnp.dot(source, weight_rows, preferred_element_type=jnp.float32)  23.8 us
    ppermute x1, waiting for transfers between devices, on_device(): x_new = jax.lax.ppermute(x_new, 'seq', all_rows)  16.7 us
    all_gather x1, blocking collectives, on_device(): lax.all_gather(values_mem, 'seq', axis=0, tiled=True)  16.4 us
  transfers between devices with their start and end apart: 7, of which 5 were waited for; matrix products, arithmetic and copies ran while one was open for 9% of the time, Pallas kernels for 0%

profile of v1, /device:TPU:0, one launch (start us, length us, event | category | flops | bytes accessed | tf_op | source)
XLA Modules:
  0.0 284.1 jit_solution(3277889132892866081)
XLA Ops:
  6.5 0.0 all-gather.11.cloned.1.call-start
  6.5 1.5 copy.64
  8.0 0.0 copy-start.1
  8.0 1.6 copy.65
  9.6 1.7 fusion.18
  11.3 0.0 all-gather.11.cloned.1.call-update
  11.3 0.0 all-gather.5.cloned.1.call-start
  11.4 0.7 all-gather.5.cloned.1.call-update
  12.1 0.0 copy-start.5
  12.1 0.0 copy-start.4
  12.1 0.0 all-gather.9.cloned.1.call-start
  12.1 0.7 all-gather.9.cloned.1.call-update
  12.8 0.0 all-gather.7.cloned.1.call-start
  12.9 0.5 all-gather.7.cloned.1.call-update
  13.4 0.0 copy-done.1
  13.4 3.1 %collective-permute-start = (bf16[1024,512]{1,0:T(8,128)(2,1)S(1)}, bf16[1024,512]{1,0:T(8,128)(2,1)S(1)}, u32[]{:S(2)}, u32[]{:S(2)}) collective-permute-start(bf16[1024,512]{1,0:T(8,128)(2,1)S(1)} %copy-done.1), channel_id=1, source_target_pairs={{0,4},{4,8},{8,12},{12,0},{1,5},{5,9},{9,13},{13,1},{2,6},{6,10},{... | collective-permute-start | bytes 3145736 | tf_op jit(solution)/shard_map/ppermute | solution.py:119
  16.5 2.1 collective-permute-start.1
  18.6 2.2 broadcast_in_dim.75
  20.8 1.1 constant_dynamic-update-slice_fusion.3
  21.9 0.0 copy-done.5
  21.9 0.1 select_reduce_fusion
  22.0 0.1 dynamic_slice.3
  22.8 19.8 %collective-permute-done = bf16[1024,512]{1,0:T(8,128)(2,1)S(1)} collective-permute-done((bf16[1024,512]{1,0:T(8,128)(2,1)S(1)}, bf16[1024,512]{1,0:T(8,128)(2,1)S(1)}, u32[]{:S(2)}, u32[]{:S(2)}) %collective-permute-start) | collective-permute-done | bytes 1048608 | tf_op jit(solution)/shard_map/ppermute | solution.py:119
  42.6 0.0 collective-permute-start.2
  42.6 0.6 fusion.42
  43.2 0.0 copy-done.4
  43.2 1.3 fusion.33
  44.5 1.3 broadcast_select_fusion
  45.8 0.2 broadcast_compare_fusion
  46.0 1.0 constant_dynamic-update-slice_fusion.2
  47.1 16.7 %collective-permute-done.1 = bf16[1024,512]{1,0:T(8,128)(2,1)S(1)} collective-permute-done((bf16[1024,512]{1,0:T(8,128)(2,1)S(1)}, bf16[1024,512]{1,0:T(8,128)(2,1)S(1)}, u32[]{:S(2)}, u32[]{:S(2)}) %collective-permute-start.1) | collective-permute-done | bytes 1048608 | tf_op jit(solution)/shard_map/ppermute | solution.py:124
  63.8 1.0 constant_dynamic-update-slice_fusion.1
  64.9 29.4 %collective-permute-done.2 = bf16[1024,512]{1,0:T(8,128)(2,1)S(1)} collective-permute-done((bf16[1024,512]{1,0:T(8,128)(2,1)S(1)}, bf16[1024,512]{1,0:T(8,128)(2,1)S(1)}, u32[]{:S(2)}, u32[]{:S(2)}) %collective-permute-start.2) | collective-permute-done | bytes 1048608 | tf_op jit(solution)/shard_map/ppermute | solution.py:119
  94.2 1.0 constant_dynamic-update-slice_fusion
  95.3 0.0 all-gather.11.cloned.1.call-done
  95.3 3.3 %convolution_convert_fusion.4 = bf16[128,512]{1,0:T(8,128)(2,1)S(1)} fusion(bf16[128,4096]{0,1:T(8,128)(2,1)} %all-gather.11.cloned.1.call-done, bf16[4096,512]{1,0:T(8,128)(2,1)} %constant_dynamic-update-slice_fusion), kind=kOutput, calls=%fused_computation.24 | convolution fusion | flops 536936448 | bytes 5373952 | tf_op jit(solution)/shard_map/dot_general | solution.py:24
  98.6 31.2 %all_gather.22 = bf16[512,512]{1,0:T(8,128)(2,1)} all-gather(bf16[128,512]{1,0:T(8,128)(2,1)S(1)} %convolution_convert_fusion.4), channel_id=1, replica_groups=mesh['groups'=2,'seq'=4,'tensor'=2,'sub'=2] {'seq'}, dimensions={0}, use_global_device_ids=true | all-gather | bytes 655360 | tf_op jit(solution)/shard_map/all_gather | solution.py:143
  129.8 0.0 all-gather.5.cloned.1.call-done
  129.8 5.9 %fusion.17 = bf16[512,512]{0,1:T(8,128)(2,1)S(1)} fusion(bf16[4096,512]{1,0:T(8,128)(2,1)} %constant_dynamic-update-slice_fusion, bf16[512,4096]{1,0:T(8,128)(2,1)} %all-gather.5.cloned.1.call-done), kind=kOutput, calls=%fused_computation.21 | convolution fusion | flops 2147745792 | bytes 8912896 | tf_op jit(solution)/shard_map/dot_general | solution.py:24
  135.6 0.1 reshape_reshape.10
  135.8 27.4 %all-gather.9.cloned.1.call-done = bf16[4096,512]{1,0:T(8,128)(2,1)} async-done(((bf16[1024,512]{1,0:T(8,128)(2,1)}), bf16[4096,512]{1,0:T(8,128)(2,1)}) %all-gather.9.cloned.1.call-update) | async-done | bytes 4194320 | tf_op jit(solution)/shard_map/all_gather | solution.py:98
  163.2 5.8 %convolution_convert_fusion = bf16[512,512]{0,1:T(8,128)(2,1)S(1)} fusion(bf16[512,4096]{1,0:T(8,128)(2,1)} %all-gather.5.cloned.1.call-done, bf16[4096,512]{1,0:T(8,128)(2,1)} %all-gather.9.cloned.1.call-done), kind=kOutput, calls=%fused_computation.17 | convolution fusion | flops 2147745792 | bytes 8912896 | tf_op jit(solution)/shard_map/dot_general | solution.py:24
  169.0 0.0 copy-start.3
  169.0 0.1 reshape_reshape.11
  169.1 75.4 %all-gather.7.cloned.1.call-done = bf16[4096,512]{1,0:T(8,128)(2,1)} async-done(((bf16[1024,512]{1,0:T(8,128)(2,1)}), bf16[4096,512]{1,0:T(8,128)(2,1)}) %all-gather.7.cloned.1.call-update) | async-done | bytes 4194320 | tf_op jit(solution)/shard_map/all_gather | solution.py:128
  244.5 0.0 copy-done.3
  244.5 5.8 %convolution_convert_fusion.2 = bf16[512,512]{1,0:T(8,128)(2,1)S(1)} fusion(bf16[512,4096]{1,0:T(8,128)(2,1)} %all-gather.5.cloned.1.call-done, bf16[4096,512]{1,0:T(8,128)(2,1)} %all-gather.7.cloned.1.call-done), kind=kOutput, calls=%fused_computation.19 | convolution fusion | flops 2147745792 | bytes 8912896 | tf_op jit(solution)/shard_map/dot_general | solution.py:24
  250.3 0.1 reshape_reshape.9
  250.4 0.5 fusion.43
  251.0 0.3 fusion.9
  251.3 0.0 copy-start
  251.3 0.5 convolution_bitcast_fusion
  251.8 0.3 copy.49
  252.1 0.3 copy.54
  252.5 0.0 copy-done
  252.5 3.0 %convolution_convert_fusion.3 = bf16[128,512]{1,0:T(8,128)(2,1)S(1)} fusion(bf16[128,4096]{0,1:T(8,128)(2,1)S(1)} %copy-done, bf16[4096,512]{1,0:T(8,128)(2,1)} %all-gather.7.cloned.1.call-done), kind=kOutput, calls=%fused_computation.23 | convolution fusion | flops 536936448 | bytes 5373952 | tf_op jit(solution)/shard_map/dot_general | solution.py:24
  255.5 16.4 %all_gather.23 = bf16[512,512]{1,0:T(8,128)(2,1)S(1)} all-gather(bf16[128,512]{1,0:T(8,128)(2,1)S(1)} %convolution_convert_fusion.3), channel_id=1, replica_groups=mesh['groups'=2,'seq'=4,'tensor'=2,'sub'=2] {'seq'}, dimensions={0}, use_global_device_ids=true | all-gather | bytes 655360 | tf_op jit(solution)/shard_map/all_gather | solution.py:144
  271.9 0.2 copy.62
  272.1 0.0 copy-done.2
  272.1 1.9 fusion.2
  274.0 0.9 fusion
  274.9 1.4 fusion.23
  276.4 0.2 copy.57
  276.6 1.0 select_convert_fusion
  (5 shorter events, 0.0 us)
Async XLA Ops:
  6.5 88.7 %all-gather.11.cloned.1.call-start = ((), (), s32[]{:S(2)}) async-start(), calls=%async_computation.3 | async-start | bytes 1310720 | tf_op jit(solution)/shard_map/all_gather | solution.py:90
  8.0 5.4 %copy-start.1 = (bf16[1024,512]{1,0:T(8,128)(2,1)S(1)}, bf16[1024,512]{1,0:T(8,128)(2,1)}, u32[]{:S(2)}) copy-start(bf16[1024,512]{1,0:T(8,128)(2,1)} %param.12) | copy-start | bytes 3145732
  11.3 118.4 %all-gather.5.cloned.1.call-start = ((), (), s32[]{:S(2)}) async-start(), calls=%async_computation | async-start | bytes 5242880 | tf_op jit(solution)/shard_map/all_gather | solution.py:89
  12.1 9.8 %copy-start.5 = (s32[8]{0:T(128)S(1)}, s32[8]{0:T(128)}, u32[]{:S(2)}) copy-start(s32[8]{0:T(128)} %param.14) | copy-start | bytes 100
  12.1 31.1 %copy-start.4 = (pred[512]{0:T(512)(128)(4,1)S(1)}, pred[512]{0:T(512)(128)(4,1)}, u32[]{:S(2)}) copy-start(pred[512]{0:T(512)(128)(4,1)} %constant.187) | copy-start | bytes 1540
  12.1 151.1 %all-gather.9.cloned.1.call-start = ((), (), s32[]{:S(2)}) async-start(), calls=%async_computation.2 | async-start | bytes 5242880 | tf_op jit(solution)/shard_map/all_gather | solution.py:98
  12.8 231.7 %all-gather.7.cloned.1.call-start = ((), (), s32[]{:S(2)}) async-start(), calls=%async_computation.1 | async-start | bytes 5242880 | tf_op jit(solution)/shard_map/all_gather | solution.py:128
  13.4 29.1 %collective-permute-start = (bf16[1024,512]{1,0:T(8,128)(2,1)S(1)}, bf16[1024,512]{1,0:T(8,128)(2,1)S(1)}, u32[]{:S(2)}, u32[]{:S(2)}) collective-permute-start(bf16[1024,512]{1,0:T(8,128)(2,1)S(1)} %copy-done.1), channel_id=1, source_target_pairs={{0,4},{4,8},{8,12},{12,0},{1,5},{5,9},{9,13},{13,1},{2,6},{6,10},{... | collective-permute-start | bytes 3145736 | tf_op jit(solution)/shard_map/ppermute | solution.py:119
  16.5 47.3 %collective-permute-start.1 = (bf16[1024,512]{1,0:T(8,128)(2,1)S(1)}, bf16[1024,512]{1,0:T(8,128)(2,1)S(1)}, u32[]{:S(2)}, u32[]{:S(2)}) collective-permute-start(bf16[1024,512]{1,0:T(8,128)(2,1)S(1)} %copy-done.1), channel_id=1, source_target_pairs={{0,12},{4,0},{8,4},{12,8},{1,13},{5,1},{9,5},{13,9},{2,14},{6,2},{... | collective-permute-start | bytes 3145736 | tf_op jit(solution)/shard_map/ppermute | solution.py:124
  42.6 51.7 %collective-permute-start.2 = (bf16[1024,512]{1,0:T(8,128)(2,1)S(1)}, bf16[1024,512]{1,0:T(8,128)(2,1)S(1)}, u32[]{:S(2)}, u32[]{:S(2)}) collective-permute-start(bf16[1024,512]{1,0:T(8,128)(2,1)S(1)} %collective-permute-done), channel_id=1, source_target_pairs={{0,4},{4,8},{8,12},{12,0},{1,5},{5,9},{9,13},{13,1},{2,6},{6,10},{... | collective-permute-start | bytes 3145736 | tf_op jit(solution)/shard_map/ppermute | solution.py:119
  169.0 75.5 %copy-start.3 = (bf16[512,512]{0,1:T(8,128)(2,1)}, bf16[512,512]{0,1:T(8,128)(2,1)S(1)}, u32[]{:S(2)}) copy-start(bf16[512,512]{0,1:T(8,128)(2,1)S(1)} %convolution_convert_fusion) | copy-start | bytes 1572868
  251.3 1.2 copy-start
  252.5 19.6 %copy-start.2 = (bf16[512,512]{1,0:T(8,128)(2,1)S(1)}, bf16[512,512]{1,0:T(8,128)(2,1)}, u32[]{:S(2)}) copy-start(bf16[512,512]{1,0:T(8,128)(2,1)} %all_gather.22) | copy-start | bytes 1572868
Sparse Core Ops, SparseCore 0:
  11.4 19.4 all-gather.10
  32.5 34.4 all-gather.4
  68.6 94.5 all-gather.8
  164.6 79.8 all-gather.6
